TPU v7x, 256 devices: a whole 4x4x8 slice. The times are simulated.
256 devices in a mesh: pipe: 8 (over x, core), seq: 8 (over z), tensor: 4 (over y).
Axes of the slice: x: 4, y: 4, z: 8, core: 2. Of those that a mesh axis runs over, the one named last changes fastest.
Arguments:
- hidden: bfloat16 [8, 1024, 14336], P('pipe', 'seq', 'tensor'), may hold values from -6 to 6
- down_weight: bfloat16 [8, 14336, 8192], P('pipe', 'tensor', 'seq'), may hold values from -0.046875 to 0.046875
- resid: bfloat16 [1024, 8192], P('tensor', 'seq'), may hold values from -42 to 42
- target: bfloat16 [1024, 8192], P('tensor', 'seq'), may hold values from -6 to 6
- gain: float32 [8192], P('seq'), may hold values from 0.1 to 1.9
- query_left: float32 [8, 8192, 32], P('pipe', 'seq'), may hold values from -0.0625 to 0.0625
- query_right: bfloat16 [8, 14336, 32], P('pipe', 'tensor'), may hold values from -0.046875 to 0.046875
- query_core: float32 [8, 1024], P('pipe'), may hold values from -6 to 6
- eigen: float32 [8, 1024], P('pipe'), may hold values from 0.1 to 10
- lengths: int32 [32], replicated, may hold values from 1 to 256, 1024 in all
Outputs:
- scores: float32 [32], P(('seq', 'tensor'))
All inputs are finite; a program needn't handle non-finite values.
Results may differ from a plain program's by a relative error of at most 0.0006.
Values may be sent and summed in bfloat16 or wider, within the bound.
No kernel may reach another device: no remote copies, remote signals or barrier semaphores. Data moves between devices by JAX's collectives and lax.ppermute only.
A program may use at most 64 MiB of HBM per device.

v0:
```python
import jax
import jax.numpy as jnp
from jax import lax
from jax.sharding import PartitionSpec as P

D = 8192


def per_device(
    hidden, down_weight, resid, target, gain, query_left, query_right, query_core, eigen, lengths
):
    tensor_count = lax.axis_size("tensor")
    gathered = lax.all_gather(hidden[0], "seq", axis=0, tiled=True)
    total_rows = gathered.shape[0]
    block_rows = total_rows // tensor_count
    weight = down_weight[0]
    right_partial = jnp.dot(gathered, query_right[0], preferred_element_type=jnp.float32)
    partial_value = lax.psum_scatter(
        jnp.dot(gathered, weight, preferred_element_type=jnp.float32).astype(jnp.bfloat16),
        "tensor",
        scatter_dimension=0,
        tiled=True,
    ).astype(jnp.float32)
    summed = lax.psum(partial_value, "pipe")
    stream = resid.astype(jnp.float32) + summed
    weighted_target = gain[None, :] * target.astype(jnp.float32)
    square_sum, inner = lax.psum(
        (jnp.sum(stream * stream, axis=1), jnp.sum(weighted_target * stream, axis=1)), "seq"
    )
    root = jnp.sqrt(square_sum / D + 1e-05)
    grad_stream = (
        weighted_target / root[:, None] - stream * (inner / (D * root * root * root))[:, None]
    )
    left_proj = jnp.dot(grad_stream, query_left[0], precision=lax.Precision.HIGHEST)
    right_proj = lax.psum_scatter(right_partial, "tensor", scatter_dimension=0, tiled=True)
    rank_width = left_proj.shape[1]
    outer = (left_proj[:, :, None] * right_proj[:, None, :]).reshape(
        block_rows, rank_width * rank_width
    )
    ends = jnp.cumsum(lengths)
    starts = ends - lengths
    token = lax.axis_index("tensor") * block_rows + jnp.arange(block_rows, dtype=jnp.int32)
    member = ((token[None, :] >= starts[:, None]) & (token[None, :] < ends[:, None])).astype(
        jnp.float32
    )
    partial_cores = jnp.dot(member, outer, precision=lax.Precision.HIGHEST)
    cores = lax.psum_scatter(partial_cores, ("seq", "tensor"), scatter_dimension=0, tiled=True)
    scaled = cores / eigen[0][None, :]
    score_term = jnp.sum(query_core[0][None, :] * scaled, axis=1)
    self_term = jnp.sum(cores * scaled, axis=1)
    score_total, self_total = lax.psum((score_term, self_term), "pipe")
    return score_total / jnp.sqrt(self_total + 1e-06)


def solution(mesh):
    placed = (
        P("pipe", "seq", "tensor"),
        P("pipe", "tensor", "seq"),
        P("tensor", "seq"),
        P("tensor", "seq"),
        P("seq"),
        P("pipe", "seq", None),
        P("pipe", "tensor", None),
        P("pipe", None),
        P("pipe", None),
        P(),
    )
    return jax.shard_map(
        per_device, mesh=mesh, in_specs=placed, out_specs=P(("seq", "tensor")), check_vma=False
    )
```

profile of v0, /device:TPU:1, one launch (start us, length us, event | category | flops | bytes accessed | tf_op | source)
XLA Modules:
  0.0 375.0 jit_solution(16374362809391073880)
XLA Ops:
  6.5 0.7 all-gather.3.cloned.1.call-update
  7.3 0.0 reduce-scatter.3.cloned.1.call-start
  7.3 90.0 %all-gather.3.cloned.1.call-done = bf16[1,1024,3584]{2,1,0:T(8,128)(2,1)} async-done(((bf16[1,128,3584]{2,1,0:T(8,128)(2,1)}), bf16[1,1024,3584]{2,1,0:T(8,128)(2,1)}) %all-gather.3.cloned.1.call-update) | async-done | bytes 7340048 | tf_op jit(solution)/shard_map/all_gather | solution.py:13
  97.3 13.3 %fusion.5 = bf16[1024,1024]{1,0:T(8,128)(2,1)} fusion(bf16[1,3584,1024]{2,1,0:T(8,128)(2,1)} %param.11, bf16[1,1024,3584]{2,1,0:T(8,128)(2,1)} %all-gather.3.cloned.1.call-done), kind=kOutput, calls=%fused_computation.5 | convolution fusion | flops 7517241344 | bytes 16777216 | tf_op jit(solution)/shard_map/dot_general | solution.py:19
  110.6 0.0 reduce-scatter.3.cloned.1.call-update
  110.6 0.0 reduce-scatter.5.cloned.1.call-start
  110.7 0.1 copy.15
  110.8 0.1 reduce-window.8
  110.8 0.1 reduce.2
  111.0 6.0 %fusion.2 = f32[1024,32]{0,1:T(8,128)} fusion(bf16[1,1024,3584]{2,1,0:T(8,128)(2,1)} %all-gather.3.cloned.1.call-done, bf16[1,3584,32]{1,2,0:T(8,128)(2,1)S(1)} %copy-done), kind=kOutput, calls=%fused_computation.2 | convolution fusion | flops 234881024 | bytes 7700480 | tf_op jit(solution)/shard_map/dot_general | solution.py:17
  116.9 0.0 reduce-scatter.5.cloned.1.call-update
  117.0 0.0 all-reduce.6.cloned.1.call-start
  117.0 24.6 %reduce-scatter.3.cloned.1.call-done = bf16[256,1024]{1,0:T(8,128)(2,1)} async-done(((bf16[1024,1024]{1,0:T(8,128)(2,1)}), bf16[256,1024]{1,0:T(8,128)(2,1)}) %reduce-scatter.3.cloned.1.call-update) | async-done | bytes 524304 | tf_op jit(solution)/shard_map/reduce_scatter | solution.py:18
  141.7 50.4 %all-reduce.7 = f32[256,1024]{1,0:T(8,128)S(1)} all-reduce(bf16[256,1024]{1,0:T(8,128)(2,1)} %reduce-scatter.3.cloned.1.call-done), channel_id=1, replica_groups=mesh['pipe'=8,'seq'=8,'tensor'=4] {'pipe'}, use_global_device_ids=true, to_apply=%region_2.0 | all-reduce | flops 262144 | bytes 1572864 | tf_op jit(solution)/shard_map/psum | solution.py:24
  192.1 0.4 multiply_reduce_fusion.1
  192.5 13.7 %all-reduce.1 = (f32[256]{0:T(256)S(1)}, f32[256]{0:T(256)S(1)}) all-reduce(f32[256]{0:T(256)S(1)} %get-tuple-element.6, f32[256]{0:T(256)S(1)} %get-tuple-element.5), channel_id=1, replica_groups=mesh['pipe'=8,'seq'=8,'tensor'=4] {'seq'}, use_global_device_ids=true, to_apply=%region_6.0 | all-reduce | flops 512 | bytes 4096 | tf_op jit(solution)/shard_map/psum | solution.py:27
  206.2 1.2 fusion.10
  207.4 0.0 reduce-scatter.5.cloned.1.call-done
  207.5 0.9 broadcast_multiply_fusion
  208.3 1.3 fusion.19
  209.7 0.6 dynamic-slice
  210.3 137.4 %all-reduce.6.cloned.1.call-done = f32[32,1024]{1,0:T(8,128)} async-done(((f32[32,1024]{1,0:T(8,128)}), f32[32,1024]{1,0:T(8,128)}) %all-reduce.6.cloned.1.call-update) | async-done | bytes 131088
  347.7 2.0 multiply_reduce_fusion.2
  349.7 16.9 %all-reduce.2 = (f32[1]{0:T(128)}, f32[1]{0:T(128)}) all-reduce(f32[1]{0:T(128)} %bitcast.6, f32[1]{0:T(128)} %bitcast.7), channel_id=1, replica_groups=mesh['pipe'=8,'seq'=8,'tensor'=4] {'pipe'}, use_global_device_ids=true, to_apply=%region_10.11 | all-reduce | flops 2 | bytes 16 | tf_op jit(solution)/shard_map/psum | solution.py:51
  (23 shorter events, 0.1 us)
Async XLA Ops:
  6.5 104.4 %copy-start = (bf16[1,3584,32]{1,2,0:T(8,128)(2,1)S(1)}, bf16[1,3584,32]{1,2,0:T(8,128)(2,1)}, u32[]{:S(2)}) copy-start(bf16[1,3584,32]{1,2,0:T(8,128)(2,1)} %param.16) | copy-start | bytes 688132
  6.5 90.8 %all-gather.3.cloned.1.call-start = ((), (), s32[]{:S(2)}) async-start(), calls=%async_computation.4 | async-start | bytes 8257536 | tf_op jit(solution)/shard_map/all_gather | solution.py:13
  7.3 103.4 %copy-start.6 = (s32[32]{0:T(128)S(1)}, s32[32]{0:T(128)}, u32[]{:S(2)}) copy-start(s32[32]{0:T(128)} %param.19) | copy-start | bytes 388
  7.3 134.4 %reduce-scatter.3.cloned.1.call-start = ((), (), s32[]{:S(2)}) async-start(), calls=%async_computation.2 | async-start | bytes 2621440 | tf_op jit(solution)/shard_map/reduce_scatter | solution.py:18
  110.6 81.5 %copy-start.1 = (bf16[256,1024]{1,0:T(8,128)(2,1)S(1)}, bf16[256,1024]{1,0:T(8,128)(2,1)}, u32[]{:S(2)}) copy-start(bf16[256,1024]{1,0:T(8,128)(2,1)} %param.13) | copy-start | bytes 1572868
  110.6 81.5 %copy-start.2 = (bf16[256,1024]{1,0:T(8,128)(2,1)S(1)}, bf16[256,1024]{1,0:T(8,128)(2,1)}, u32[]{:S(2)}) copy-start(bf16[256,1024]{1,0:T(8,128)(2,1)} %param.12) | copy-start | bytes 1572868
  110.6 81.5 %copy-start.3 = (f32[1024]{0:T(1024)S(1)}, f32[1024]{0:T(1024)}, u32[]{:S(2)}) copy-start(f32[1024]{0:T(1024)} %param.14) | copy-start | bytes 12292
  110.6 95.6 %copy-start.7 = (f32[1,1024,32]{1,2,0:T(8,128)S(1)}, f32[1,1024,32]{1,2,0:T(8,128)}, u32[]{:S(2)}) copy-start(f32[1,1024,32]{1,2,0:T(8,128)} %param.15) | copy-start | bytes 393220
  110.6 96.9 %reduce-scatter.5.cloned.1.call-start = ((), (), s32[]{:S(2)}) async-start(), calls=%async_computation.3 | async-start | bytes 163840 | tf_op jit(solution)/shard_map/reduce_scatter | solution.py:35
  116.9 92.8 %copy-start.8 = (u32[256]{0:T(256)S(1)}, u32[256]{0:T(256)}, u32[]{:S(2)}) copy-start(u32[256]{0:T(256)} %constant.28) | copy-start | bytes 3076
  116.9 230.7 %copy-start.4 = (f32[1,1024]{1,0:T(1,128)S(1)}, f32[1,1024]{1,0:T(1,128)}, u32[]{:S(2)}) copy-start(f32[1,1024]{1,0:T(1,128)} %param.17) | copy-start | bytes 12292
  116.9 230.7 %copy-start.5 = (f32[1,1024]{1,0:T(1,128)S(1)}, f32[1,1024]{1,0:T(1,128)}, u32[]{:S(2)}) copy-start(f32[1,1024]{1,0:T(1,128)} %param.18) | copy-start | bytes 12292
  117.0 230.7 %all-reduce.6.cloned.1.call-start = ((), (), s32[]{:S(2)}) async-start(), calls=%async_computation.5 | async-start | bytes 262144
Sparse Core Ops, SparseCore 0:
  9.1 88.1 all-gather.2
  110.7 30.8 reduce-scatter.2
  144.3 20.4 reduce-scatter.4
  209.8 137.8 all-reduce.5
where the time goes:
time: 375 us
  waiting for transfers between devices  253 us (67%)
  blocking collectives  81 us (22%)
  matrix products  21.7 us (6%)
  between operations  15.1 us (4%)
    unnamed x5, waiting for transfers between devices  138 us
    all_gather x1, waiting for transfers between devices, per_device(): gathered = lax.all_gather(hidden[0], 'seq', axis=0, tiled=True)  90 us
    psum x1, blocking collectives, per_device(): summed = lax.psum(partial_value, 'pipe')  50.4 us
    reduce_scatter x1, waiting for transfers between devices, per_device(): lax.psum_scatter(jnp.dot(gathered, weight, preferred_element_type=jnp.flo...  24.6 us
    psum x1, blocking collectives, per_device(): score_total, self_total = lax.psum((score_term, self_term), 'pipe')  16.9 us
    psum x1, blocking collectives, per_device(): lax.psum((jnp.sum(stream * stream, axis=1), jnp.sum(weighted_target * str...  13.7 us
    dot_general x1, matrix products, per_device(): jnp.dot(gathered, weight, preferred_element_type=jnp.float32)  13.3 us
  transfers between devices with their start and end apart: 4, of which 3 were waited for; matrix products, arithmetic and copies ran while one was open for 2% of the time, Pallas kernels for 0%

commit v1 on v0

--- a/solution.py
+++ b/solution.py
@@ -10,7 +10,11 @@
     hidden, down_weight, resid, target, gain, query_left, query_right, query_core, eigen, lengths
 ):
     tensor_count = lax.axis_size("tensor")
-    gathered = lax.all_gather(hidden[0], "seq", axis=0, tiled=True)
+    part = hidden[0]
+    count = lax.axis_size("seq")
+    pieces = jnp.stack([part for _ in range(count)])
+    pieces = lax.all_to_all(pieces, "seq", split_axis=0, concat_axis=0)
+    gathered = jnp.concatenate(pieces, axis=0)
     total_rows = gathered.shape[0]
     block_rows = total_rows // tensor_count
     weight = down_weight[0]

time: 375 us -> 456 us (1.22)
  blocking collectives: 81 us -> 252 us
  waiting for transfers between devices: 253 us -> 162 us
  local copies, waits for them, and re-layouts: 0.71 us -> 5.63 us
    all_to_all x0 -> x1, blocking collectives: none -> 171 us  [per_device(): pieces = lax.all_to_all(pieces, 'seq', split_axis=0, concat_axis=0)]
    all_gather x1 -> x0, waiting for transfers between devices: 90 us -> none  [per_device(): gathered = lax.all_gather(hidden[0], 'seq', axis=0, tiled=True)]
    unnamed x5 -> x4, waiting for transfers between devices: 138 us -> 137 us
  transfers between devices with their start and end apart: 4 -> 3, of which waited for: 3 -> 2; matrix products, arithmetic and copies ran while one was open for 2% -> 2% of each run, Pallas kernels for 0% -> 0%
where the time goes in v1:
time: 456 us
  blocking collectives  252 us (55%)
  waiting for transfers between devices  162 us (36%)
  matrix products  17.5 us (4%)
  between operations  15.1 us (3%)
  local copies, waits for them, and re-layouts  5.63 us (1%)
    all_to_all x1, blocking collectives, per_device(): pieces = lax.all_to_all(pieces, 'seq', split_axis=0, concat_axis=0)  171 us
    unnamed x4, waiting for transfers between devices  137 us
    psum x1, blocking collectives, per_device(): summed = lax.psum(partial_value, 'pipe')  50.4 us
    reduce_scatter x1, waiting for transfers between devices, per_device(): lax.psum_scatter(jnp.dot(gathered, weight, preferred_element_type=jnp.flo...  24.2 us
    psum x1, blocking collectives, per_device(): score_total, self_total = lax.psum((score_term, self_term), 'pipe')  16.9 us
    psum x1, blocking collectives, per_device(): lax.psum((jnp.sum(stream * stream, axis=1), jnp.sum(weighted_target * str...  13.7 us
  transfers between devices with their start and end apart: 3, of which 2 were waited for; matrix products, arithmetic and copies ran while one was open for 2% of the time, Pallas kernels for 0%

profile of v1, /device:TPU:1, one launch (start us, length us, event | category | flops | bytes accessed | tf_op | source)
XLA Modules:
  0.0 455.6 jit_solution(6347826501617459759)
XLA Ops:
  6.5 1.9 stack.3
  8.5 171.1 %all_to_all.5 = bf16[8,128,3584]{2,1,0:T(8,128)(2,1)S(1)} all-to-all(bf16[8,128,3584]{2,1,0:T(8,128)(2,1)S(1)} %stack.3), channel_id=1, replica_groups=mesh['pipe'=8,'seq'=8,'tensor'=4] {'seq'}, dimensions={0} | all-to-all | bytes 14680064 | tf_op jit(solution)/shard_map/all_to_all | solution.py:16
  179.6 3.0 copy-done.1
  182.6 9.0 %fusion.2 = bf16[1024,1024]{1,0:T(8,128)(2,1)} fusion(bf16[1024,3584]{1,0:T(8,128)(2,1)S(1)} %bitcast.21, bf16[1,3584,1024]{2,1,0:T(8,128)(2,1)S(1)} %bitcast.27), kind=kOutput, calls=%fused_computation.2 | convolution fusion | flops 7517241344 | bytes 16777216 | tf_op jit(solution)/shard_map/dot_general | solution.py:23
  191.6 0.0 reduce-scatter.3.cloned.1.call-update
  191.6 0.0 reduce-scatter.5.cloned.1.call-start
  191.7 0.1 copy.15
  191.8 0.1 reduce-window.8
  191.9 0.1 reduce.2
  192.0 6.0 %fusion.12 = f32[1024,32]{0,1:T(8,128)} fusion(bf16[1024,3584]{1,0:T(8,128)(2,1)} %bitcast.22, bf16[1,3584,32]{1,2,0:T(8,128)(2,1)S(1)} %copy-done), kind=kOutput, calls=%fused_computation.15 | convolution fusion | flops 234881024 | bytes 7700480 | tf_op jit(solution)/shard_map/dot_general | solution.py:21
  198.0 0.0 reduce-scatter.5.cloned.1.call-update
  198.0 0.0 all-reduce.6.cloned.1.call-start
  198.0 24.2 %reduce-scatter.3.cloned.1.call-done = bf16[256,1024]{1,0:T(8,128)(2,1)} async-done(((bf16[1024,1024]{1,0:T(8,128)(2,1)}), bf16[256,1024]{1,0:T(8,128)(2,1)}) %reduce-scatter.3.cloned.1.call-update) | async-done | bytes 524304 | tf_op jit(solution)/shard_map/reduce_scatter | solution.py:22
  222.2 50.4 %all-reduce.7 = f32[256,1024]{1,0:T(8,128)S(1)} all-reduce(bf16[256,1024]{1,0:T(8,128)(2,1)} %reduce-scatter.3.cloned.1.call-done), channel_id=1, replica_groups=mesh['pipe'=8,'seq'=8,'tensor'=4] {'pipe'}, use_global_device_ids=true, to_apply=%region_2.0 | all-reduce | flops 262144 | bytes 1572864 | tf_op jit(solution)/shard_map/psum | solution.py:28
  272.7 0.4 multiply_reduce_fusion.1
  273.0 13.7 %all-reduce.1 = (f32[256]{0:T(256)S(1)}, f32[256]{0:T(256)S(1)}) all-reduce(f32[256]{0:T(256)S(1)} %get-tuple-element.6, f32[256]{0:T(256)S(1)} %get-tuple-element.5), channel_id=1, replica_groups=mesh['pipe'=8,'seq'=8,'tensor'=4] {'seq'}, use_global_device_ids=true, to_apply=%region_6.0 | all-reduce | flops 512 | bytes 4096 | tf_op jit(solution)/shard_map/psum | solution.py:31
  286.8 1.2 fusion.5
  288.0 0.0 reduce-scatter.5.cloned.1.call-done
  288.0 0.9 broadcast_multiply_fusion
  288.9 1.3 fusion.15
  290.2 0.6 dynamic-slice
  290.8 137.4 %all-reduce.6.cloned.1.call-done = f32[32,1024]{1,0:T(8,128)} async-done(((f32[32,1024]{1,0:T(8,128)}), f32[32,1024]{1,0:T(8,128)}) %all-reduce.6.cloned.1.call-update) | async-done | bytes 131088
  428.3 2.0 multiply_reduce_fusion.2
  430.3 16.9 %all-reduce.2 = (f32[1]{0:T(128)}, f32[1]{0:T(128)}) all-reduce(f32[1]{0:T(128)} %bitcast.7, f32[1]{0:T(128)} %bitcast.8), channel_id=1, replica_groups=mesh['pipe'=8,'seq'=8,'tensor'=4] {'pipe'}, use_global_device_ids=true, to_apply=%region_10.11 | all-reduce | flops 2 | bytes 16 | tf_op jit(solution)/shard_map/psum | solution.py:55
  (29 shorter events, 0.1 us)
Async XLA Ops:
  6.5 185.5 %copy-start = (bf16[1,3584,32]{1,2,0:T(8,128)(2,1)S(1)}, bf16[1,3584,32]{1,2,0:T(8,128)(2,1)}, u32[]{:S(2)}) copy-start(bf16[1,3584,32]{1,2,0:T(8,128)(2,1)} %param.16) | copy-start | bytes 688132
  6.5 215.7 %reduce-scatter.3.cloned.1.call-start = ((), (), s32[]{:S(2)}) async-start(), calls=%async_computation.3 | async-start | bytes 2621440 | tf_op jit(solution)/shard_map/reduce_scatter | solution.py:22
  6.5 176.1 %slice-start = ((s8[7340032]{0:T(1024)(128)(4,1)}), s8[4194304]{0:T(1024)(128)(4,1)S(1)}, s32[]{:S(2)}) async-start(s8[7340032]{0:T(1024)(128)(4,1)} %bitcast.26), calls=%async_computation.6 | async-start | bytes 8388608
  8.5 174.1 %slice-start.1 = ((s8[7340032]{0:T(1024)(128)(4,1)}), s8[3145728]{0:T(1024)(128)(4,1)S(1)}, s32[]{:S(2)}) async-start(s8[7340032]{0:T(1024)(128)(4,1)} %bitcast.26), calls=%async_computation.7 | async-start | bytes 6291456
  179.6 3.0 copy-start.1
  182.6 9.1 %copy-start.7 = (s32[32]{0:T(128)S(1)}, s32[32]{0:T(128)}, u32[]{:S(2)}) copy-start(s32[32]{0:T(128)} %param.19) | copy-start | bytes 388
  191.6 81.0 %copy-start.2 = (bf16[256,1024]{1,0:T(8,128)(2,1)S(1)}, bf16[256,1024]{1,0:T(8,128)(2,1)}, u32[]{:S(2)}) copy-start(bf16[256,1024]{1,0:T(8,128)(2,1)} %param.13) | copy-start | bytes 1572868
  191.6 81.1 %copy-start.3 = (bf16[256,1024]{1,0:T(8,128)(2,1)S(1)}, bf16[256,1024]{1,0:T(8,128)(2,1)}, u32[]{:S(2)}) copy-start(bf16[256,1024]{1,0:T(8,128)(2,1)} %param.12) | copy-start | bytes 1572868
  191.6 81.1 %copy-start.4 = (f32[1024]{0:T(1024)S(1)}, f32[1024]{0:T(1024)}, u32[]{:S(2)}) copy-start(f32[1024]{0:T(1024)} %param.14) | copy-start | bytes 12292
  191.6 95.2 %copy-start.8 = (f32[1,1024,32]{1,2,0:T(8,128)S(1)}, f32[1,1024,32]{1,2,0:T(8,128)}, u32[]{:S(2)}) copy-start(f32[1,1024,32]{1,2,0:T(8,128)} %param.15) | copy-start | bytes 393220
  191.6 96.4 %reduce-scatter.5.cloned.1.call-start = ((), (), s32[]{:S(2)}) async-start(), calls=%async_computation.4 | async-start | bytes 163840 | tf_op jit(solution)/shard_map/reduce_scatter | solution.py:39
  198.0 92.3 %copy-start.9 = (u32[256]{0:T(256)S(1)}, u32[256]{0:T(256)}, u32[]{:S(2)}) copy-start(u32[256]{0:T(256)} %constant.28) | copy-start | bytes 3076
  198.0 230.3 %copy-start.5 = (f32[1,1024]{1,0:T(1,128)S(1)}, f32[1,1024]{1,0:T(1,128)}, u32[]{:S(2)}) copy-start(f32[1,1024]{1,0:T(1,128)} %param.17) | copy-start | bytes 12292
  198.0 230.3 %copy-start.6 = (f32[1,1024]{1,0:T(1,128)S(1)}, f32[1,1024]{1,0:T(1,128)}, u32[]{:S(2)}) copy-start(f32[1,1024]{1,0:T(1,128)} %param.18) | copy-start | bytes 12292
  198.0 230.3 %all-reduce.6.cloned.1.call-start = ((), (), s32[]{:S(2)}) async-start(), calls=%async_computation.5 | async-start | bytes 262144
Sparse Core Ops, SparseCore 0:
  191.8 30.4 reduce-scatter.2
  224.9 20.5 reduce-scatter.4
  290.4 137.8 all-reduce.5
